TPU v7x, 512 devices: a whole 4x8x8 slice. The times are simulated.
512 devices in a mesh: gx: 16 (over x, z_hi), gy: 32 (over y, z_lo, core).
Axes of the slice: x: 4, y: 8, z: 8 (z_hi: 4, z_lo: 2; z = z_hi * 2 + z_lo), core: 2. Of those that a mesh axis runs over, the one named last changes fastest.
Arguments:
- prev_block: float32 [3, 8, 128, 256, 128], P(None, None, 'gx', 'gy'), may hold values from -20 to 20
- block: float32 [3, 8, 128, 256, 128], P(None, None, 'gx', 'gy'), may hold values from -20 to 20
- hop_seed: int32 [3, 128, 256, 128], P(None, 'gx', 'gy'), may hold values from 0 to 15
- levels: int32 [128, 256, 128], P('gx', 'gy'), may hold values from 0 to 15
- hop_table: float32 [3, 16, 3, 3], replicated, may hold values from -3 to 3
- onsite_table: float32 [16, 3], replicated, may hold values from -2 to 2
Outputs:
- next_block: float32 [3, 8, 128, 256, 128], P(None, None, 'gx', 'gy')
- alpha: float32 [8, 8], replicated
- beta: float32 [8, 8], replicated
All inputs are finite; a program needn't handle non-finite values.
Results may differ from a plain program's by a relative error of at most 0.0003.
Values sent between devices are 32-bit elements; how exact they have to be, the bound alone decides.
A program may use at most 64 MiB of HBM per device.

v0:
```python
import jax
import jax.numpy as jnp
from jax import lax
from jax.sharding import PartitionSpec as P

HIGH = lax.Precision.HIGHEST


def extended(value, sides, width):
    for axis, dim in sides:
        count, length = (lax.axis_size(axis), value.shape[dim])
        up = [(i, (i + 1) % count) for i in range(count)]
        down = [(j, i) for i, j in up]
        last = lax.slice_in_dim(value, length - width, length, axis=dim)
        leading = lax.slice_in_dim(value, 0, width, axis=dim)
        before = lax.ppermute(last, axis, up)
        after = lax.ppermute(leading, axis, down)
        value = jnp.concatenate([before, value, after], axis=dim)
    return value


def passed_along(value, axis, steps):
    count = lax.axis_size(axis)
    pairs = [(source, (source + steps) % count) for source in range(count)]
    return lax.ppermute(value, axis, pairs)


def table_rows(table_flat, indices):
    entries = table_flat.shape[0]
    flat = indices.reshape(-1)
    onehot = (flat[None, :] == jnp.arange(entries, dtype=jnp.int32)[:, None]).astype(jnp.float32)
    picked = lax.dot_general(table_flat, onehot, (((0,), (0,)), ((), ())), precision=HIGH)
    return picked.reshape((table_flat.shape[1],) + indices.shape)


def hop_blocks(table_dir, seeds):
    orbs = table_dir.shape[1]
    picked = table_rows(table_dir.reshape(table_dir.shape[0], orbs * orbs), seeds)
    return picked.reshape((orbs, orbs) + seeds.shape)


def forward(bonds, field):
    orbs = field.shape[0]
    rows = []
    for left in range(orbs):
        acc = bonds[left, 0][None] * field[0]
        for right in range(1, orbs):
            acc = acc + bonds[left, right][None] * field[right]
        rows.append(acc)
    return jnp.stack(rows, axis=0)


def backward(bonds, field):
    orbs = field.shape[0]
    rows = []
    for right in range(orbs):
        acc = bonds[0, right][None] * field[0]
        for left in range(1, orbs):
            acc = acc + bonds[left, right][None] * field[left]
        rows.append(acc)
    return jnp.stack(rows, axis=0)


def onsite_image(block, levels, onsite_table):
    energy = table_rows(onsite_table, levels)
    return energy[:, None] * block


def apply_values(block, hop_seed, levels, hop_table, onsite_table):
    padded = extended(block, (("gx", 2), ("gy", 3)), 1)
    ahead = [padded[:, :, 2:, 1:-1], padded[:, :, 1:-1, 2:], jnp.roll(block, -1, axis=4)]
    behind = [padded[:, :, :-2, 1:-1], padded[:, :, 1:-1, :-2], jnp.roll(block, 1, axis=4)]
    edge_x = passed_along(hop_seed[0, -1:], "gx", 1)
    edge_y = passed_along(hop_seed[1, :, -1:], "gy", 1)
    seeds_behind = [
        jnp.concatenate([edge_x, hop_seed[0, :-1]], axis=0),
        jnp.concatenate([edge_y, hop_seed[1, :, :-1]], axis=1),
        jnp.roll(hop_seed[2], 1, axis=2),
    ]
    image = onsite_image(block, levels, onsite_table)
    for direction in range(3):
        image = image + forward(
            hop_blocks(hop_table[direction], hop_seed[direction]), ahead[direction]
        )
        image = image + backward(
            hop_blocks(hop_table[direction], seeds_behind[direction]), behind[direction]
        )
    return image


def local_inner(left, right):
    total = None
    for orbit in range(left.shape[0]):
        flat_left = left[orbit].reshape(left.shape[1], -1)
        flat_right = right[orbit].reshape(right.shape[1], -1)
        part_sum = lax.dot_general(flat_left, flat_right, (((1,), (1,)), ((), ())), precision=HIGH)
        total = part_sum if total is None else total + part_sum
    return total


def apply_left(matrix, field):
    rows = []
    for orbit in range(field.shape[0]):
        flat = field[orbit].reshape(field.shape[1], -1)
        mixed = jnp.dot(matrix, flat, precision=HIGH)
        rows.append(mixed.reshape((matrix.shape[0],) + field.shape[2:]))
    return jnp.stack(rows, axis=0)


def combine(basis, coeffs):
    return apply_left(coeffs.T, basis)


def per_device(prev_block, block, hop_seed, levels, hop_table, onsite_table):
    count = (
        block.shape[0]
        * block.shape[2]
        * block.shape[3]
        * block.shape[4]
        * lax.axis_size("gx")
        * lax.axis_size("gy")
    )
    product = apply_values(block, hop_seed, levels, hop_table, onsite_table)
    basis = jnp.concatenate([prev_block, block], axis=1)
    width = block.shape[1]
    first = lax.psum(local_inner(basis, product), ("gx", "gy")) / count
    residual_one = product - combine(basis, first)
    second = lax.psum(local_inner(basis, residual_one), ("gx", "gy")) / count
    residual_two = residual_one - combine(basis, second)
    gram = lax.psum(local_inner(residual_two, residual_two), ("gx", "gy")) / count
    alpha = first[width:]
    lower = jnp.linalg.cholesky(gram)
    lower_inv = jax.scipy.linalg.solve_triangular(
        lower, jnp.eye(width, dtype=jnp.float32), lower=True
    )
    next_block = apply_left(lower_inv, residual_two)
    return (next_block, alpha, lower.T)


def solution(mesh):
    in_specs = (
        P(None, None, "gx", "gy", None),
        P(None, None, "gx", "gy", None),
        P(None, "gx", "gy", None),
        P("gx", "gy", None),
        P(),
        P(),
    )
    out_specs = (P(None, None, "gx", "gy", None), P(), P())
    return jax.shard_map(
        per_device, mesh=mesh, in_specs=in_specs, out_specs=out_specs, check_vma=False
    )
```

profile of v0, /device:TPU:1, one launch (start us, length us, event | category | flops | bytes accessed | tf_op | source)
XLA Modules:
  0.0 391.7 jit_solution(6826044836774343264)
XLA Ops:
  0.7 1.0 fusion.80
  2.3 6.6 %collective-permute-start.2 = (f32[3,8,1,8,128]{4,1,3,2,0:T(8,128)}, f32[3,8,1,8,128]{4,1,3,2,0:T(8,128)}, u32[]{:S(2)}, u32[]{:S(2)}) collective-permute-start(f32[3,8,1,8,128]{4,1,3,2,0:T(8,128)} %copy.105), channel_id=1, source_target_pairs={{0,32},{32,64},{64,96},{96,128},{128,160},{160,192},{192,224},{224... | collective-permute-start | bytes 294920 | tf_op jit(solution)/shard_map/ppermute | solution.py:16
  9.6 9.0 %collective-permute-start = (f32[3,8,1,8,128]{4,1,3,2,0:T(8,128)}, f32[3,8,1,8,128]{4,1,3,2,0:T(8,128)}, u32[]{:S(2)}, u32[]{:S(2)}) collective-permute-start(f32[3,8,1,8,128]{4,1,3,2,0:T(8,128)} %copy.104), channel_id=1, source_target_pairs={{32,0},{64,32},{96,64},{128,96},{160,128},{192,160},{224,192},{256... | collective-permute-start | bytes 294920 | tf_op jit(solution)/shard_map/ppermute | solution.py:17
  18.6 1.4 slice.453
  20.0 3.9 %collective-permute-start.4 = (s32[8,1,128]{2,0,1:T(8,128)}, s32[8,1,128]{2,0,1:T(8,128)}, u32[]{:S(2)}, u32[]{:S(2)}) collective-permute-start(s32[8,1,128]{2,0,1:T(8,128)} %bitcast.37), channel_id=1, source_target_pairs={{0,1},{1,2},{2,3},{3,4},{4,5},{5,6},{6,7},{7,8},{8,9},{9,10},{10,1... | collective-permute-start | bytes 12296 | tf_op jit(solution)/shard_map/ppermute | solution.py:25
  23.9 1.3 slice_bitcast_fusion.72
  25.2 1.9 collective-permute-start.1
  27.1 0.8 slice_bitcast_fusion.69
  27.9 1.1 fusion.79
  29.1 1.2 fusion.78
  32.9 1.6 copy.108
  34.5 1.3 copy.109
  36.3 0.7 slice_bitcast_fusion.26
  37.0 1.4 copy.106
  38.4 1.3 copy.107
  40.7 0.7 slice_bitcast_fusion.44
  42.6 1.8 multiply_add_fusion.2
  44.5 1.4 multiply_add_fusion.1
  46.0 1.1 multiply_add_fusion.4
  49.9 0.9 constant_dynamic-update-slice_fusion.6
  51.4 0.9 constant_dynamic-update-slice_fusion.4
  52.3 0.7 fusion.77
  53.1 1.9 collective-permute-start.3
  55.0 3.8 collective-permute-start.5
  58.8 1.1 fusion.76
  60.0 1.1 multiply_add_fusion.17
  61.0 1.0 multiply_add_fusion.14
  62.4 1.2 copy.45
  63.6 0.9 reshape_squeeze.22
  64.5 1.1 copy.83
  65.7 2.0 copy.47
  67.7 1.9 reshape_squeeze.23
  69.6 2.0 copy.84
  71.8 1.2 multiply_add_fusion.8
  75.3 0.9 fusion.10
  76.3 0.7 convolution_bitcast_fusion.16
  77.0 0.8 fusion.3
  77.8 0.8 fusion.2
  78.6 101.8 %psum.21 = f32[16,8]{0,1:T(8,128)S(1)} all-reduce(f32[16,8]{0,1:T(8,128)S(1)} %fusion.2), channel_id=1, replica_groups=mesh['gx'=16,'gy'=32] {'gx','gy'}, use_global_device_ids=true, to_apply=%region_0.1 | all-reduce | flops 128 | bytes 1024 | tf_op jit(solution)/shard_map/psum | solution.py:126
  182.5 2.7 maximum_subtract_fusion
  185.3 0.7 convolution_bitcast_fusion.13
  186.0 0.8 fusion.1
  186.8 0.8 fusion
  187.6 94.6 %psum.22 = f32[16,8]{0,1:T(8,128)S(1)} all-reduce(f32[16,8]{0,1:T(8,128)S(1)} %fusion), channel_id=1, replica_groups=mesh['gx'=16,'gy'=32] {'gx','gy'}, use_global_device_ids=true, to_apply=%region_1.2 | all-reduce | flops 128 | bytes 1024 | tf_op jit(solution)/shard_map/psum | solution.py:128
  283.6 1.7 convolution_bitcast_fusion
  285.3 3.5 maximum_subtract_fusion.1
  290.8 94.3 %psum.23 = f32[8,8]{0,1:T(8,128)S(1)} all-reduce(f32[8,8]{0,1:T(8,128)S(1)} %fusion.5), channel_id=1, replica_groups=mesh['gx'=16,'gy'=32] {'gx','gy'}, use_global_device_ids=true, to_apply=%region_2.3 | all-reduce | flops 64 | bytes 512 | tf_op jit(solution)/shard_map/psum | solution.py:130
  389.3 1.0 copy.57
  (217 shorter events, 22.9 us)
Async XLA Ops:
  0.6 46.5 %copy-start = (f32[16,3]{0,1:T(4,128)S(1)}, f32[16,3]{0,1:T(4,128)}, u32[]{:S(2)}) copy-start(f32[16,3]{0,1:T(4,128)} %param.11) | copy-start | bytes 580
  0.6 27.3 %copy-start.1 = (f32[3,8,8,8,128]{4,3,2,1,0:T(8,128)S(1)}, f32[3,8,8,8,128]{4,3,2,1,0:T(8,128)}, u32[]{:S(2)}) copy-start(f32[3,8,8,8,128]{4,3,2,1,0:T(8,128)} %param.7) | copy-start | bytes 2359300
  2.3 47.6 %collective-permute-start.2 = (f32[3,8,1,8,128]{4,1,3,2,0:T(8,128)}, f32[3,8,1,8,128]{4,1,3,2,0:T(8,128)}, u32[]{:S(2)}, u32[]{:S(2)}) collective-permute-start(f32[3,8,1,8,128]{4,1,3,2,0:T(8,128)} %copy.105), channel_id=1, source_target_pairs={{0,32},{32,64},{64,96},{96,128},{128,160},{160,192},{192,224},{224... | collective-permute-start | bytes 294920 | tf_op jit(solution)/shard_map/ppermute | solution.py:16
  9.6 41.8 %collective-permute-start = (f32[3,8,1,8,128]{4,1,3,2,0:T(8,128)}, f32[3,8,1,8,128]{4,1,3,2,0:T(8,128)}, u32[]{:S(2)}, u32[]{:S(2)}) collective-permute-start(f32[3,8,1,8,128]{4,1,3,2,0:T(8,128)} %copy.104), channel_id=1, source_target_pairs={{32,0},{64,32},{96,64},{128,96},{160,128},{192,160},{224,192},{256... | collective-permute-start | bytes 294920 | tf_op jit(solution)/shard_map/ppermute | solution.py:17
  20.0 27.5 %collective-permute-start.4 = (s32[8,1,128]{2,0,1:T(8,128)}, s32[8,1,128]{2,0,1:T(8,128)}, u32[]{:S(2)}, u32[]{:S(2)}) collective-permute-start(s32[8,1,128]{2,0,1:T(8,128)} %bitcast.37), channel_id=1, source_target_pairs={{0,1},{1,2},{2,3},{3,4},{4,5},{5,6},{6,7},{7,8},{8,9},{9,10},{10,1... | collective-permute-start | bytes 12296 | tf_op jit(solution)/shard_map/ppermute | solution.py:25
  25.2 24.2 %collective-permute-start.1 = (s32[1,8,128]{2,1,0:T(8,128)}, s32[1,8,128]{2,1,0:T(8,128)S(1)}, u32[]{:S(2)}, u32[]{:S(2)}) collective-permute-start(s32[1,8,128]{2,1,0:T(8,128)} %slice_bitcast_fusion.72), channel_id=1, source_target_pairs={{0,32},{32,64},{64,96},{96,128},{128,160},{160,192},{192,224},{224... | collective-permute-start | bytes 12296 | tf_op jit(solution)/shard_map/ppermute | solution.py:25
  29.1 2.5 copy-start.71
  32.1 2.3 copy-start.34
  37.0 2.7 copy-start.40
  41.9 2.5 copy-start.3
  41.9 2.4 copy-start.4
  41.9 2.4 copy-start.54
  42.0 2.4 copy-start.55
  42.0 2.4 copy-start.56
  42.0 2.4 copy-start.63
  42.0 2.4 copy-start.64
  42.0 2.4 copy-start.65
  45.9 2.2 copy-start.69
  47.4 2.0 copy-start.67
  52.3 7.6 %copy-start.38 = (f32[3,8,10,8,128]{4,1,3,2,0:T(8,128)}, f32[3,8,10,8,128]{4,1,3,2,0:T(8,128)S(1)}, u32[]{:S(2)}) copy-start(f32[3,8,10,8,128]{4,1,3,2,0:T(8,128)S(1)} %get-tuple-element.112) | copy-start | bytes 2949124
  53.1 18.6 %collective-permute-start.3 = (f32[3,8,10,1,128]{4,1,3,2,0:T(8,128)}, f32[3,8,10,1,128]{4,1,3,2,0:T(8,128)}, u32[]{:S(2)}, u32[]{:S(2)}) collective-permute-start(f32[3,8,10,1,128]{4,1,3,2,0:T(8,128)} %get-tuple-element.33), channel_id=1, source_target_pairs={{1,0},{2,1},{3,2},{4,3},{5,4},{6,5},{7,6},{8,7},{9,8},{10,9},{11,1... | collective-permute-start | bytes 368648 | tf_op jit(solution)/shard_map/ppermute | solution.py:17
  55.0 16.7 %collective-permute-start.5 = (f32[3,8,10,1,128]{4,1,3,2,0:T(8,128)}, f32[3,8,10,1,128]{4,1,3,2,0:T(8,128)}, u32[]{:S(2)}, u32[]{:S(2)}) collective-permute-start(f32[3,8,10,1,128]{4,1,3,2,0:T(8,128)} %get-tuple-element.32), channel_id=1, source_target_pairs={{0,1},{1,2},{2,3},{3,4},{4,5},{5,6},{6,7},{7,8},{8,9},{9,10},{10,1... | collective-permute-start | bytes 368648 | tf_op jit(solution)/shard_map/ppermute | solution.py:16
  69.6 2.0 copy-start.39
  71.8 1.8 copy-start.27
  73.0 3.3 copy-start.28
  73.0 3.3 copy-start.29
  73.1 1.9 copy-start.21
  73.1 2.0 copy-start.23
  73.1 2.1 copy-start.24
  73.1 2.1 copy-start.25
  73.1 2.2 copy-start.26
  73.5 2.7 copy-start.30
  73.6 2.7 copy-start.31
  73.6 2.7 copy-start.32
  73.6 2.7 copy-start.33
  180.4 2.1 copy-start.7
  180.4 2.1 copy-start.10
  180.4 2.1 copy-start.13
  180.4 2.1 copy-start.16
  180.4 2.1 copy-start.18
  180.4 2.1 copy-start.20
  180.4 2.1 copy-start.22
  181.1 4.2 %copy-start.35 = (f32[1,8,8,8,128]{4,1,3,2,0:T(8,128)}, f32[1,8,8,8,128]{4,1,3,2,0:T(8,128)S(1)}, u32[]{:S(2)}) copy-start(f32[1,8,8,8,128]{4,1,3,2,0:T(8,128)S(1)} %convolution_bitcast_fusion.5) | copy-start | bytes 786436
  181.8 3.5 copy-start.36
  182.5 2.8 copy-start.37
  187.6 97.7 %copy-start.8 = (f32[1,8,8,8,128]{4,1,3,2,0:T(8,128)S(1)}, f32[1,8,8,8,128]{4,1,3,2,0:T(8,128)}, u32[]{:S(2)}) copy-start(f32[1,8,8,8,128]{4,1,3,2,0:T(8,128)} %get-tuple-element.9) | copy-start | bytes 786436
  187.6 97.7 %copy-start.11 = (f32[1,8,8,8,128]{4,1,3,2,0:T(8,128)S(1)}, f32[1,8,8,8,128]{4,1,3,2,0:T(8,128)}, u32[]{:S(2)}) copy-start(f32[1,8,8,8,128]{4,1,3,2,0:T(8,128)} %get-tuple-element.21) | copy-start | bytes 786436
  187.6 97.7 %copy-start.14 = (f32[1,8,8,8,128]{4,1,3,2,0:T(8,128)S(1)}, f32[1,8,8,8,128]{4,1,3,2,0:T(8,128)}, u32[]{:S(2)}) copy-start(f32[1,8,8,8,128]{4,1,3,2,0:T(8,128)} %get-tuple-element.22) | copy-start | bytes 786436
  (30 other events, 43.1 us)
where the time goes:
time: 393 us; the launch traced here: 392 us
  blocking collectives  291 us (74%)
  local copies, waits for them, and re-layouts  38 us (10%)
  starting transfers between devices  27.2 us (7%)
  other arithmetic  18.6 us (5%)
  matrix products  15.1 us (4%)
    psum x1, blocking collectives, per_device(): first = lax.psum(local_inner(basis, product), ('gx', 'gy')) / count  102 us
    psum x1, blocking collectives, per_device(): second = lax.psum(local_inner(basis, residual_one), ('gx', 'gy')) / count  94.6 us
    psum x1, blocking collectives, per_device(): lax.psum(local_inner(residual_two, residual_two), ('gx', 'gy')) / count  94.3 us
    unnamed x171, local copies, waits for them, and re-layouts  17.2 us
    ppermute x2, starting transfers between devices, extended(): after = lax.ppermute(leading, axis, down)  10.9 us
    ppermute x2, starting transfers between devices, extended(): before = lax.ppermute(last, axis, up)  10.5 us
  transfers between devices with their start and end apart: 6, of which 0 were waited for; matrix products, arithmetic and copies ran while one was open for 10% of the time, Pallas kernels for 0%

commit v1 on v0

--- a/solution.py
+++ b/solution.py
@@ -125,7 +125,7 @@
     width = block.shape[1]
     first = lax.psum(local_inner(basis, product), ("gx", "gy")) / count
     residual_one = product - combine(basis, first)
-    second = lax.psum(local_inner(basis, residual_one), ("gx", "gy")) / count
+    second = jnp.sum(lax.all_gather(local_inner(basis, residual_one), ("gx", "gy")), axis=0) / count
     residual_two = residual_one - combine(basis, second)
     gram = lax.psum(local_inner(residual_two, residual_two), ("gx", "gy")) / count
     alpha = first[width:]

time: 393 us -> 984 us (2.50)
  blocking collectives: 291 us -> 880 us
    all_gather x0 -> x1, blocking collectives: none -> 684 us  [per_device(): lax.all_gather(local_inner(basis, residual_one), ('gx', 'gy'))]
    psum x1 -> x0, blocking collectives: 94.6 us -> none  [per_device(): second = lax.psum(local_inner(basis, residual_one), ('gx', 'gy')) / count]
  transfers between devices with their start and end apart: 6 -> 6, of which waited for: 0 -> 0; matrix products, arithmetic and copies ran while one was open for 10% -> 4% of each run, Pallas kernels for 0% -> 0%
where the time goes in v1:
time: 984 us; the launch traced here: 983 us
  blocking collectives  880 us (89%)
  local copies, waits for them, and re-layouts  40 us (4%)
  starting transfers between devices  27.2 us (3%)
  other arithmetic  18.9 us (2%)
  matrix products  15.1 us (2%)
    all_gather x1, blocking collectives, per_device(): lax.all_gather(local_inner(basis, residual_one), ('gx', 'gy'))  684 us
    psum x1, blocking collectives, per_device(): first = lax.psum(local_inner(basis, product), ('gx', 'gy')) / count  102 us
    psum x1, blocking collectives, per_device(): lax.psum(local_inner(residual_two, residual_two), ('gx', 'gy')) / count  93.9 us
  transfers between devices with their start and end apart: 6, of which 0 were waited for; matrix products, arithmetic and copies ran while one was open for 4% of the time, Pallas kernels for 0%

profile of v1, /device:TPU:1, one launch (start us, length us, event | category | flops | bytes accessed | tf_op | source)
XLA Modules:
  0.0 983.1 jit_solution(11507515158405790461)
XLA Ops:
  0.7 1.0 fusion.81
  2.3 6.6 collective-permute-start.2
  9.6 9.0 collective-permute-start
  18.6 1.4 slice.453
  20.0 3.9 collective-permute-start.4
  23.9 1.3 slice_bitcast_fusion.72
  25.2 1.9 collective-permute-start.1
  27.1 0.8 slice_bitcast_fusion.69
  27.9 1.1 fusion.80
  29.1 1.2 fusion.79
  32.8 1.6 copy.138
  34.4 1.3 copy.139
  37.0 1.3 copy.136
  38.3 1.3 copy.137
  40.6 0.7 slice_bitcast_fusion.44
  42.5 1.8 multiply_add_fusion.2
  44.4 1.4 multiply_add_fusion.1
  45.9 1.2 multiply_add_fusion.4
  48.5 0.7 slice_bitcast_fusion.35
  49.8 0.9 constant_dynamic-update-slice_fusion.6
  51.3 0.9 constant_dynamic-update-slice_fusion.4
  52.2 0.8 fusion.78
  53.0 1.9 collective-permute-start.3
  54.9 3.8 collective-permute-start.5
  58.7 1.1 fusion.77
  59.8 1.1 multiply_add_fusion.17
  60.9 1.1 multiply_add_fusion.14
  62.1 0.9 reshape_squeeze.21
  63.0 1.1 copy.112
  64.2 1.2 copy.75
  65.4 0.9 reshape_squeeze.22
  66.3 1.1 copy.113
  67.5 2.2 copy.77
  69.7 1.9 reshape_squeeze.23
  71.6 2.0 copy.114
  73.8 1.2 multiply_add_fusion.8
  77.4 0.8 fusion.11
  79.0 0.8 fusion.4
  79.7 0.8 fusion.3
  80.5 101.8 %psum.14 = f32[16,8]{0,1:T(8,128)S(1)} all-reduce(f32[16,8]{0,1:T(8,128)S(1)} %fusion.3), channel_id=1, replica_groups=mesh['gx'=16,'gy'=32] {'gx','gy'}, use_global_device_ids=true, to_apply=%region_0.1 | all-reduce | flops 128 | bytes 1024 | tf_op jit(solution)/shard_map/psum | solution.py:126
  184.5 2.9 maximum_subtract_fusion
  188.1 0.8 fusion.2
  188.8 0.8 fusion.1
  189.6 684.2 %all-gather.1 = f32[512,16,8]{1,2,0:T(8,128)S(1)} all-gather(f32[1,16,8]{1,2,0:T(8,128)S(1)} %fusion.1), channel_id=2, replica_groups=mesh['gx'=16,'gy'=32] {'gx','gy'}, dimensions={0}, use_global_device_ids=true | all-gather | bytes 262656 | tf_op jit(solution)/shard_map/all_gather | solution.py:128
  875.1 1.7 convolution_bitcast_fusion.1
  877.5 3.1 maximum_subtract_fusion.1
  882.7 93.9 %psum.15 = f32[8,8]{0,1:T(8,128)S(1)} all-reduce(f32[8,8]{0,1:T(8,128)S(1)} %fusion.6), channel_id=1, replica_groups=mesh['gx'=16,'gy'=32] {'gx','gy'}, use_global_device_ids=true, to_apply=%region_2.3 | all-reduce | flops 64 | bytes 512 | tf_op jit(solution)/shard_map/psum | solution.py:130
  980.7 1.0 copy.87
  (224 shorter events, 24.8 us)
Async XLA Ops:
  0.6 46.4 %copy-start = (f32[16,3]{0,1:T(4,128)S(1)}, f32[16,3]{0,1:T(4,128)}, u32[]{:S(2)}) copy-start(f32[16,3]{0,1:T(4,128)} %param.11) | copy-start | bytes 580
  0.6 27.3 %copy-start.1 = (f32[3,8,8,8,128]{4,3,2,1,0:T(8,128)S(1)}, f32[3,8,8,8,128]{4,3,2,1,0:T(8,128)}, u32[]{:S(2)}) copy-start(f32[3,8,8,8,128]{4,3,2,1,0:T(8,128)} %param.7) | copy-start | bytes 2359300
  2.3 47.5 %collective-permute-start.2 = (f32[3,8,1,8,128]{4,1,3,2,0:T(8,128)}, f32[3,8,1,8,128]{4,1,3,2,0:T(8,128)}, u32[]{:S(2)}, u32[]{:S(2)}) collective-permute-start(f32[3,8,1,8,128]{4,1,3,2,0:T(8,128)} %copy.135), channel_id=1, source_target_pairs={{0,32},{32,64},{64,96},{96,128},{128,160},{160,192},{192,224},{224... | collective-permute-start | bytes 294920 | tf_op jit(solution)/shard_map/ppermute | solution.py:16
  9.6 41.7 %collective-permute-start = (f32[3,8,1,8,128]{4,1,3,2,0:T(8,128)}, f32[3,8,1,8,128]{4,1,3,2,0:T(8,128)}, u32[]{:S(2)}, u32[]{:S(2)}) collective-permute-start(f32[3,8,1,8,128]{4,1,3,2,0:T(8,128)} %copy.134), channel_id=1, source_target_pairs={{32,0},{64,32},{96,64},{128,96},{160,128},{192,160},{224,192},{256... | collective-permute-start | bytes 294920 | tf_op jit(solution)/shard_map/ppermute | solution.py:17
  20.0 27.4 %collective-permute-start.4 = (s32[8,1,128]{2,0,1:T(8,128)}, s32[8,1,128]{2,0,1:T(8,128)}, u32[]{:S(2)}, u32[]{:S(2)}) collective-permute-start(s32[8,1,128]{2,0,1:T(8,128)} %bitcast.37), channel_id=1, source_target_pairs={{0,1},{1,2},{2,3},{3,4},{4,5},{5,6},{6,7},{7,8},{8,9},{9,10},{10,1... | collective-permute-start | bytes 12296 | tf_op jit(solution)/shard_map/ppermute | solution.py:25
  25.2 24.1 %collective-permute-start.1 = (s32[1,8,128]{2,1,0:T(8,128)}, s32[1,8,128]{2,1,0:T(8,128)S(1)}, u32[]{:S(2)}, u32[]{:S(2)}) collective-permute-start(s32[1,8,128]{2,1,0:T(8,128)} %slice_bitcast_fusion.72), channel_id=1, source_target_pairs={{0,32},{32,64},{64,96},{96,128},{128,160},{160,192},{192,224},{224... | collective-permute-start | bytes 12296 | tf_op jit(solution)/shard_map/ppermute | solution.py:25
  29.1 2.5 copy-start.74
  32.1 2.3 copy-start.40
  37.0 2.7 copy-start.46
  41.9 2.4 copy-start.3
  41.9 2.4 copy-start.4
  41.9 2.4 copy-start.66
  41.9 2.4 copy-start.67
  41.9 2.4 copy-start.68
  45.8 2.2 copy-start.72
  47.3 2.0 copy-start.70
  52.2 7.6 copy-start.44
  53.0 20.7 %collective-permute-start.3 = (f32[3,8,10,1,128]{4,1,3,2,0:T(8,128)}, f32[3,8,10,1,128]{4,1,3,2,0:T(8,128)}, u32[]{:S(2)}, u32[]{:S(2)}) collective-permute-start(f32[3,8,10,1,128]{4,1,3,2,0:T(8,128)} %get-tuple-element.36), channel_id=1, source_target_pairs={{1,0},{2,1},{3,2},{4,3},{5,4},{6,5},{7,6},{8,7},{9,8},{10,9},{11,1... | collective-permute-start | bytes 368648 | tf_op jit(solution)/shard_map/ppermute | solution.py:17
  54.9 18.8 %collective-permute-start.5 = (f32[3,8,10,1,128]{4,1,3,2,0:T(8,128)}, f32[3,8,10,1,128]{4,1,3,2,0:T(8,128)}, u32[]{:S(2)}, u32[]{:S(2)}) collective-permute-start(f32[3,8,10,1,128]{4,1,3,2,0:T(8,128)} %get-tuple-element.35), channel_id=1, source_target_pairs={{0,1},{1,2},{2,3},{3,4},{4,5},{5,6},{6,7},{7,8},{8,9},{9,10},{10,1... | collective-permute-start | bytes 368648 | tf_op jit(solution)/shard_map/ppermute | solution.py:16
  67.5 115.6 %copy-start.5 = (f32[2,8,64,128]{3,2,1,0:T(8,128)}, f32[2,8,64,128]{3,2,1,0:T(8,128)S(1)}, u32[]{:S(2)}) copy-start(f32[2,8,64,128]{3,2,1,0:T(8,128)S(1)} %copy.113) | copy-start | bytes 1572868
  71.6 2.1 copy-start.45
  75.0 3.1 copy-start.34
  75.1 3.1 copy-start.35
  75.1 2.1 copy-start.30
  75.2 2.1 copy-start.31
  75.2 2.2 copy-start.32
  75.6 2.6 copy-start.36
  75.6 2.6 copy-start.37
  75.6 2.6 copy-start.38
  75.6 2.6 copy-start.39
  182.3 2.1 copy-start.9
  182.3 2.1 copy-start.12
  182.3 2.1 copy-start.15
  182.3 2.1 copy-start.18
  182.3 2.1 copy-start.21
  182.3 2.1 copy-start.24
  182.3 2.1 copy-start.27
  183.0 4.3 copy-start.41
  183.7 3.6 copy-start.42
  184.4 2.9 copy-start.43
  874.3 2.4 copy-start.7
  874.3 3.1 copy-start.10
  874.3 3.1 copy-start.13
  874.3 3.1 copy-start.16
  874.4 3.1 copy-start.19
  874.4 3.1 copy-start.22
  874.4 3.1 copy-start.25
  874.4 3.1 copy-start.28
  (33 other events, 49.0 us)
